TPU v7x, 128 devices: a whole 4x4x4 slice. The times are simulated.
128 devices in a mesh: space: 16 (over z, y_hi, core), tm: 8 (over y_lo, x).
Axes of the slice: x: 4, y: 4 (y_hi: 2, y_lo: 2; y = y_hi * 2 + y_lo), z: 4, core: 2. Of those that a mesh axis runs over, the one named last changes fastest.
Arguments:
- gauge_links: float32 [4, 2, 3, 3, 32, 64, 256], P(None, None, None, None, 'tm', 'space'), may hold values from -1 to 1, as said below
Outputs:
- flowed_links: float32 [4, 2, 3, 3, 32, 64, 256], P(None, None, None, None, 'tm', 'space')
- flow_force: float32 [4, 2, 3, 3, 32, 64, 256], P(None, None, None, None, 'tm', 'space')
- holonomy: float32 [2, 3, 3, 8, 64, 256], P(None, None, None, 'tm', 'space')
Inputs may be any that keep to these rules, and one draw needn't show every extreme that they name: `gauge_links`: every link is a special unitary 3 x 3 matrix.
All inputs are finite; a program needn't handle non-finite values.
Results may differ from a plain program's by a relative error of at most 0.00002.
Values sent between devices are 32-bit elements; how exact they have to be, the bound alone decides.
No kernel may reach another device: no remote copies, remote signals or barrier semaphores. Data moves between devices by JAX's collectives and lax.ppermute only.
A program may use at most 64 MiB of HBM per device.

v0:
```python
import jax
import jax.numpy as jnp
from jax import lax
from jax.experimental import pallas as pl
from jax.experimental.pallas import tpu as pltpu
from jax.sharding import PartitionSpec as P


F32 = jnp.float32
VMEM = pltpu.VMEM
PAIRS = ((0, 1), (0, 2), (1, 2))
ROW = 4


def entry(terms):
    re = im = None
    for (ar, ai), ca, (br, bi), cb in terms:
        p = ar * br
        q = ai * bi
        re = p if re is None else re + p
        re = re + q if ca != cb else re - q
        u = ar * bi
        v = ai * br
        if im is None:
            im = (v - u) if cb and not ca else (u - v) if ca and not cb else (u + v)
        else:
            im = im - u if cb else im + u
            im = im - v if ca else im + v
    return re, im


def entry_im(terms):
    im = None
    for (ar, ai), ca, (br, bi), cb in terms:
        u = ar * bi
        v = ai * br
        if im is None:
            im = (v - u) if cb and not ca else (u - v) if ca and not cb else (u + v)
        else:
            im = im - u if cb else im + u
            im = im - v if ca else im + v
    return im


def terms(a, ha, b, hb, i, j):
    out = []
    for k in range(3):
        x = a[k][i] if ha else a[i][k]
        y = b[j][k] if hb else b[k][j]
        out.append((x, ha, y, hb))
    return out


def product(a, b, ha=False, hb=False):
    return [[entry(terms(a, ha, b, hb, i, j)) for j in range(3)] for i in range(3)]


def twice_ta(a, b):
    out = []
    for i, j in PAIRS:
        r1, i1 = entry(terms(a, False, b, False, i, j))
        r2, i2 = entry(terms(a, False, b, False, j, i))
        out += [r1 - r2, i1 + i2]
    d = [entry_im(terms(a, False, b, False, k, k)) for k in range(3)]
    tr = (d[0] + d[1] + d[2]) * (2.0 / 3.0)
    return out + [d[0] + d[0] - tr, d[1] + d[1] - tr]


def transport(u, c):
    r01, i01, r02, i02, r12, i12, d0, d1 = c
    d2 = -(d0 + d1)
    off = {(0, 1): (r01, i01), (0, 2): (r02, i02), (1, 2): (r12, i12)}
    diag = (d0, d1, d2)
    t = []
    for i in range(3):
        row = []
        for j in range(3):
            ur, ui = u[i][j]
            re = -(ui * diag[j])
            im = ur * diag[j]
            for k in range(3):
                if k == j:
                    continue
                ar, ai = u[i][k]
                if k < j:
                    cr, ci = off[k, j]
                    re = re + ar * cr - ai * ci
                    im = im + ar * ci + ai * cr
                else:
                    cr, ci = off[j, k]
                    re = re - ar * cr - ai * ci
                    im = im + ar * ci - ai * cr
            row.append((re, im))
        t.append(row)
    out = []
    for i, j in PAIRS:
        out += list(entry(terms(t, False, u, True, i, j)))
    for k in range(2):
        out.append(entry_im(terms(t, False, u, True, k, k)))
    return out


def taylor(f):
    r01, i01, r02, i02, r12, i12, h0, h1 = f
    h2 = -(h0 + h1)
    n01 = r01 * r01 + i01 * i01
    n02 = r02 * r02 + i02 * i02
    n12 = r12 * r12 + i12 * i12
    y0 = -(h0 * h0 + n01 + n02)
    y1 = -(h1 * h1 + n01 + n12)
    y2 = -(h2 * h2 + n02 + n12)
    s = 0.5 * (y0 + y1 + y2)
    y01 = (h2 * i01 - (r02 * r12 + i02 * i12), -(h2 * r01) - (i02 * r12 - r02 * i12))
    y02 = (h1 * i02 + (r01 * r12 - i01 * i12), -(h1 * r02) + (r01 * i12 + i01 * r12))
    y12 = (h0 * i12 - (r01 * r02 + i01 * i02), -(h0 * r12) - (r01 * i02 - i01 * r02))
    zr = r01 * r12 - i01 * i12
    zi = r01 * i12 + i01 * r12
    trip = zi * r02 - zr * i02
    e = -(h0 * h1 * h2 + (trip + trip) - h0 * n12 - h1 * n02 - h2 * n01)
    q0r = 1.0 - e * e * (1.0 / 720.0)
    q0i = e * (1.0 / 6.0 + s * (1.0 / 120.0))
    q1r = 1.0 + s * (1.0 / 6.0 + s * (1.0 / 120.0))
    q1i = e * (1.0 / 24.0 + s * (1.0 / 360.0))
    q2r = 0.5 + s * (1.0 / 24.0 + s * (1.0 / 720.0))
    q2i = e * (1.0 / 120.0)
    out = [[None] * 3 for _ in range(3)]
    offs = (((r01, i01), y01), ((r02, i02), y02), ((r12, i12), y12))
    for (i, j), ((xr, xi), (yr, yi)) in zip(PAIRS, offs):
        p1, p2, p3, p4 = q1r * xr, q1i * xi, q1r * xi, q1i * xr
        s1, s2, s3, s4 = q2r * yr, q2i * yi, q2r * yi, q2i * yr
        out[i][j] = ((p1 - p2) + (s1 - s2), (p3 + p4) + (s3 + s4))
        out[j][i] = ((s1 + s2) - (p1 + p2), (p3 - p4) + (s4 - s3))
    for k, (h, y) in enumerate(((h0, y0), (h1, y1), (h2, y2))):
        out[k][k] = (q0r - q1i * h + q2r * y, q0i + q1r * h + q2i * y)
    return out


def masks():
    lane = lax.broadcasted_iota(jnp.int32, (8, 128), 1)
    z = lax.broadcasted_iota(jnp.int32, (8, 128), 0) & 3
    return {"x": lane & 15, "y": lane >> 4, "z": z}


def shift_x(v, m, up):
    if up:
        return jnp.where(m["x"] == 15, pltpu.roll(v, 15, 1), pltpu.roll(v, 127, 1))
    return jnp.where(m["x"] == 0, pltpu.roll(v, 113, 1), pltpu.roll(v, 1, 1))


def shift_y(v, m, up):
    r = pltpu.roll(v, 112 if up else 16, 1)
    return jnp.where(m["y"] == (7 if up else 0), pltpu.roll(r, 4, 0), r)


def mat(fetch):
    return [[(fetch(0, i, j), fetch(1, i, j)) for j in range(3)] for i in range(3)]


def on_mat(m, f):
    return [[(f(a), f(b)) for a, b in row] for row in m]


def special(a, b, ha=False, hb=False):
    m = [[entry(terms(a, ha, b, hb, i, j)) for j in range(3)] for i in range(2)]
    return m + [third_row(m)]


def plane(u_mu, u_nu, mu_up, nu_up):
    d = special(u_mu, u_nu, ha=True)
    g = special(mu_up, nu_up, hb=True)
    return twice_ta(g, d), twice_ta(d, g)


def corner_loop(u_mu, u_nu, mu_up, nu_up, at_nu):
    d = special(u_mu, u_nu, ha=True)
    g = special(mu_up, nu_up, hb=True)
    return twice_ta(g, d) if at_nu else twice_ta(d, g)


def unpack_rows(ref, base):
    m = [[(ref[base * 12 + i * 3 + j], ref[base * 12 + 6 + i * 3 + j]) for j in range(3)] for i in range(2)]
    return m + [third_row(m)]


def third_row(m):
    third = []
    for k in range(3):
        a, b = (k + 1) % 3, (k + 2) % 3
        r1, i1 = entry([(m[0][a], False, m[1][b], False)])
        r2, i2 = entry([(m[0][b], False, m[1][a], False)])
        third.append((r1 - r2, i2 - i1))
    return third


def tiles(ref, shape):
    return ref.reshape(*shape, 8, 128)


FIRST = pl.ds(0, 8, stride=4)
LAST = pl.ds(3, 8, stride=4)


def load_kernel(u_hbm, u_ref, st_ref, lowt_ref, low_ref, high_ref, corner_ref, sem):
    two = pl.ds(0, 2)
    copy = pltpu.make_async_copy(u_hbm.at[:, :, two], u_ref.at[:, :, two], sem)
    copy.start()
    copy.wait()
    u = tiles(u_ref, (4, 2, 3, 3, 4))
    rows = u_ref.reshape(4, 2, 3, 3, 32, 128)
    for d in range(4):
        for p in range(2):
            for i in range(2):
                for j in range(3):
                    k = p * 6 + i * 3 + j
                    high_ref[d * 12 + k] = rows[d, p, i, j, LAST, :]
                    if d < 3:
                        st_ref[d * 12 + k] = u[d, p, i, j, 0]
                    if d < 2:
                        low_ref[d * 12 + k] = rows[d, p, i, j, FIRST, :]
                    if d == 3:
                        lowt_ref[k] = rows[d, p, i, j, FIRST, :]
                    if d == 2:
                        corner_ref[pl.ds(2 * k, 2), :] = rows[d, p, i, j, pl.ds(3, 2, stride=4), :]


def accumulate(ref, mu, t, vals, sign=1):
    for k in range(8):
        if sign > 0:
            ref[mu, k, t] += vals[k]
        else:
            ref[mu, k, t] -= vals[k]


def inside(vals, m):
    return [jnp.where(m["z"] == 3, 0.0, v) for v in vals]


def next_z(v):
    return pltpu.roll(v, 7, 0)


def down_z(v, m):
    return jnp.where(m["z"] == 0, 0.0, pltpu.roll(v, 1, 0))


def links(u):
    return lambda d, t: mat(lambda p, i, j: u[d, p, i, j, t])


TURNS = (shift_x, shift_y, None)


def upward(mu, v, m):
    return TURNS[mu](v, m, True) if mu < 2 else next_z(v)


def time_loops(u_t, loops, c_ref, r_ref, m, t):
    own = back = None
    for mu, (a, b) in enumerate(loops):
        down = [TURNS[mu](v, m, False) for v in b] if mu < 2 else [down_z(v, m) for v in b]
        if mu == 2:
            a, b = inside(a, m), inside(b, m)
        accumulate(c_ref, mu, t, b, -1)
        accumulate(r_ref, mu, t + 1, a)
        own = a if own is None else [v + w for v, w in zip(own, a)]
        back = down if back is None else [v + w for v, w in zip(back, down)]
    return [v - w for v, w in zip(transport(u_t, own), back)]


def steep_kernel(u_in, u_ref, c_ref, r_ref, f_ref, d_ref, up_ref):
    u = tiles(u_ref, (4, 2, 3, 3, 4))
    rows = u_ref.reshape(4, 2, 3, 3, 32, 128)

    def complete(t, carry):
        for d in range(4):
            row = third_row([[(u[d, 0, i, j, t], u[d, 1, i, j, t]) for j in range(3)] for i in range(2)])
            for j in range(3):
                for p in range(2):
                    u[d, p, 2, j, t] = row[j][p]
        return carry

    lax.fori_loop(0, 4, complete, 0)
    link = links(u)
    m = masks()
    c_ref[...] = jnp.zeros_like(c_ref)
    r_ref[...] = jnp.zeros_like(r_ref)

    def body(t, carry):
        ut = link(3, t)
        loops = (plane(link(mu, t), ut, link(mu, t + 1), on_mat(ut, lambda v: upward(mu, v, m))) for mu in range(3))
        f = time_loops(ut, loops, c_ref, r_ref, m, t)
        for k in range(8):
            f_ref[k, t] = f[k]
        return carry

    lax.fori_loop(0, 3, body, 0)
    ut = link(3, 3)
    for mu in range(3):
        put18(d_ref.at[mu], special(link(mu, 3), ut, ha=True))
        put18(up_ref.at[mu], on_mat(ut, lambda v: upward(mu, v, m)))
    put18(d_ref.at[3], special(packed(rows, 2, LAST), packed(rows, 3, LAST), ha=True))


def flat_kernel(u_ref, low_ref, high_ref, ab_ref, c_in, r_in, after_ref, c_ref, r_ref, x_ref, above_ref):
    link = links(tiles(u_ref, (4, 2, 3, 3, 4)))
    rows = u_ref.reshape(4, 2, 3, 3, 32, 128)
    m = masks()
    line = lax.broadcasted_iota(jnp.int32, (8, 128), 0)
    m["odd"] = (line & 1) == 1
    for mu in range(2):
        halo = unpack_rows(low_ref, mu)
        for i in range(3):
            for j in range(3):
                for p in range(2):
                    above_ref[mu, p, i, j, LAST, :] = halo[i][j][p]

    def body(t, carry):
        us = [link(d, t) for d in range(3)]
        a, b = plane(us[0], us[1], on_mat(us[0], lambda v: shift_y(v, m, True)), on_mat(us[1], lambda v: shift_x(v, m, True)))
        accumulate(c_ref, 1, t, a)
        accumulate(c_ref, 0, t, b, -1)
        accumulate(r_ref, 0, t, [shift_y(v, m, False) for v in a])
        accumulate(r_ref, 1, t, [shift_x(v, m, False) for v in b], -1)
        for mu, shift in ((0, shift_x), (1, shift_y)):
            up = mat(lambda p, i, j: jnp.where(m["z"] == 3, above_ref[mu, p, i, j, at(t), :], next_z(us[mu][i][j][p])))
            a, b = plane(us[mu], us[2], up, on_mat(us[2], lambda v: shift(v, m, True)))
            accumulate(c_ref, 2, t, a)
            accumulate(c_ref, mu, t, b, -1)
            accumulate(r_ref, mu, t, [down_z(v, m) for v in a])
            accumulate(r_ref, 2, t, [shift(v, m, False) for v in b], -1)
        return carry

    lax.fori_loop(0, 4, body, 0)
    uz_low = unpack_rows(high_ref, 2)
    for mu, shift in ((0, shift_x), (1, packed_shift_y)):
        a = corner_loop(unpack_rows(high_ref, mu), uz_low, packed(rows, mu, FIRST), on_mat(uz_low, lambda v: shift(v, m, True)), True)
        for k in range(8):
            expand(x_ref, 16 + mu * 8 + k, a[k], 0)
    for k in range(8):
        expand(x_ref, k, -ab_ref[8 + k], 3)
        expand(x_ref, 8 + k, jnp.where(line >= 2, pltpu.roll(ab_ref[k], 2, 0), 0.0), 3)


def expand(x_ref, n, tile, offset):
    x_ref[n] = jnp.zeros((32, 128), F32)
    x_ref[n, pl.ds(offset, 8, stride=4), :] = tile


def at(t):
    return pl.ds(t * 8 if isinstance(t, int) else pl.multiple_of(t * 8, 8), 8)


def packed_shift_y(v, m, up):
    r = pltpu.roll(v, 112 if up else 16, 1)
    other = jnp.where(m["odd"], pltpu.roll(r, 1, 0), pltpu.roll(r, 7, 0))
    return jnp.where(m["y"] == (7 if up else 0), other, r)


def packed(rows, d, part):
    return mat(lambda p, i, j: rows[d, p, i, j, part, :])


def finish(f, u, z_out, new_out):
    z = [-0.5 * v for v in f]
    zero = jnp.zeros_like(z[0])
    for n, (i, j) in enumerate(PAIRS):
        z_out(0, i, j, z[2 * n])
        z_out(1, i, j, z[2 * n + 1])
        z_out(0, j, i, -z[2 * n])
        z_out(1, j, i, z[2 * n + 1])
    for k, d in enumerate((z[6], z[7], -(z[6] + z[7]))):
        z_out(0, k, k, zero)
        z_out(1, k, k, d)
    new = product(taylor([0.125 * v for v in z]), u)
    for i in range(3):
        for j in range(3):
            for p in range(2):
                new_out(p, i, j, new[i][j][p])
    return new


def writer(ref, *head, t):
    def put(p, i, j, v):
        ref[(*head, p, i, j, t)] = v

    return put


def both_loops(d, g):
    return twice_ta(g, d), twice_ta(d, g)


def top_kernel(u_ref, ht_ref, d_ref, up_ref, c_in, r_in, f_in, c_ref, r_ref, f_ref, uz4_ref):
    ut = links(tiles(u_ref, (4, 2, 3, 3, 4)))(3, 3)
    above = [unpack_rows(ht_ref, mu) for mu in range(3)]
    put18(uz4_ref, above[2])
    loops = (both_loops(get18(d_ref.at[mu]), special(above[mu], get18(up_ref.at[mu]), hb=True)) for mu in range(3))
    f = time_loops(ut, loops, c_ref, r_ref, masks(), 3)
    for k in range(8):
        f_ref[k, 3] = f[k]


def time_kernel(u_ref, uz4_ref, lowt_ref, high_ref, corner_ref, d_ref, f_ref, r_ref, ft_ref, ab_ref, zt_ref, nt_ref, s_ref, x_ref, pk_ref, end_ref):
    link = links(tiles(u_ref, (4, 2, 3, 3, 4)))
    rows = u_ref.reshape(4, 2, 3, 3, 32, 128)
    zt, nt = tiles(zt_ref, (2, 3, 3, 4)), tiles(nt_ref, (2, 3, 3, 4))
    for p in range(2):
        for i in range(3):
            for j in range(3):
                pk_ref[p, i, j, pl.ds(0, 6), :] = rows[2, p, i, j, pl.ds(11, 6, stride=4), :]
                pk_ref[p, i, j, pl.ds(6, 2), :] = uz4_ref[p, i, j, pl.ds(3, 2, stride=4), :]
    a, b = both_loops(get18(d_ref.at[3]), special(get18(pk_ref), unpack_rows(lowt_ref, 0), hb=True))
    w = transport(packed(rows, 3, LAST), a)
    for k in range(8):
        ab_ref[k] = a[k]
        ab_ref[8 + k] = b[k]
        expand(x_ref, k, w[k], 3)
        end_ref[k] = jnp.zeros((8, 128), F32)
        end_ref[k, pl.ds(3, 2, stride=4), :] = ab_ref[k, pl.ds(6, 2), :]
    for k in range(12):
        pk_ref[k // 6, k // 3 % 2, k % 3, pl.ds(0, 6), :] = high_ref[24 + k, pl.ds(2, 6), :]
        pk_ref[k // 6, k // 3 % 2, k % 3, pl.ds(6, 2), :] = corner_ref[pl.ds(2 * k, 2), :]
    up = [[(pk_ref[0, i, j], pk_ref[1, i, j]) for j in range(3)] for i in range(2)]
    b = corner_loop(unpack_rows(high_ref, 2), unpack_rows(high_ref, 3), up + [third_row(up)], packed(rows, 3, FIRST), False)
    for k in range(8):
        x_ref[k, FIRST, :] = -b[k]
    for mu in range(3):
        for k in range(8):
            v = r_ref[mu, k, 4]
            ft_ref[mu * 8 + k] = v + end_ref[k] if mu == 2 else v

    def body(t, carry):
        u = link(3, t)
        finish([f_ref[k, t] + x_ref[k, at(t), :] for k in range(8)], u, writer(zt, t=t), writer(nt, t=t))
        return carry

    lax.fori_loop(0, 4, body, 0)
    slab = mat(lambda p, i, j: nt[p, i, j, 0])
    for t in range(1, 4):
        slab = product(slab, mat(lambda p, i, j: nt[p, i, j, t]))
    put18(s_ref, slab)


def out_copies(src, dst, sem, d, first, count):
    return [pltpu.make_async_copy(src.at[p], dst.at[d, p, :, :, pl.ds(first, count)], sem.at[p]) for p in range(2)]


def finish_space(first, count, u_ref, x_ref, c_ref, r_ref, extra, new_hbm, z_hbm, zs_ref, ns_ref, sem):
    link = links(tiles(u_ref, (4, 2, 3, 3, 4)))
    copies = []
    for mu, part in ((0, 16), (1, 24), (2, 8)):
        zs, ns = tiles(zs_ref.at[mu], (2, 3, 3, count)), tiles(ns_ref.at[mu], (2, 3, 3, count))

        def body(n, carry):
            t = first + n
            u = link(mu, t)
            c = [c_ref[mu, k, t] for k in range(8)]
            if mu == 2:
                c = [v + x_ref[k, at(t), :] for k, v in enumerate(c)]
            w = transport(u, c)
            f = [w[k] + (r_ref[mu, k, t] + x_ref[part + k, at(t), :]) for k in range(8)]
            if extra is not None:
                f = [v + extra[mu * 8 + k] for k, v in enumerate(f)]
            finish(f, u, writer(zs, t=n), writer(ns, t=n))
            return carry

        if count > 1:
            lax.fori_loop(0, count, body, 0)
        else:
            body(0, 0)
        more = out_copies(zs_ref.at[mu], z_hbm, sem.at[2 * mu], mu, first, count)
        more += out_copies(ns_ref.at[mu], new_hbm, sem.at[2 * mu + 1], mu, first, count)
        for c in more:
            c.start()
        copies += more
    return copies


def space_kernel(u_ref, x_ref, c_ref, r_ref, zt_ref, nt_ref, new_hbm, z_hbm, zs_ref, ns_ref, sem):
    copies = out_copies(zt_ref, z_hbm, sem.at[6], 3, 0, 4) + out_copies(nt_ref, new_hbm, sem.at[7], 3, 0, 4)
    for c in copies:
        c.start()
    copies += finish_space(1, 3, u_ref, x_ref, c_ref, r_ref, None, new_hbm, z_hbm, zs_ref, ns_ref, sem)
    for c in copies:
        c.wait()


def first_kernel(u_ref, x_ref, c_ref, r_ref, ft_ref, new_in, z_in, new_hbm, z_hbm, zs_ref, ns_ref, sem):
    copies = finish_space(0, 1, u_ref, x_ref, c_ref, r_ref, ft_ref, new_hbm, z_hbm, zs_ref, ns_ref, sem)
    for c in copies:
        c.wait()


def get18(ref):
    return mat(lambda p, i, j: ref[p, i, j])


def put18(ref, m):
    for i in range(3):
        for j in range(3):
            for p in range(2):
                ref[p, i, j] = m[i][j][p]


def chain(mats):
    out = mats[0]
    for x in mats[1:]:
        out = product(out, x)
    return out


def join_kernel(s0_ref, s1_ref, s2_ref, s3_ref, head_ref, tail_ref, row_ref):
    x = lax.rem(lax.axis_index("tm"), ROW)
    cyc = [s0_ref, s1_ref, s2_ref, s3_ref]
    for n in range(ROW):

        @pl.when(x == n)
        def _():
            head = chain([get18(r) for r in cyc[: ROW - n]])
            put18(head_ref, head)
            if n == 0:
                put18(row_ref, head)
                one, zero = jnp.ones((8, 128), F32), jnp.zeros((8, 128), F32)
                put18(tail_ref, [[(one if i == j else zero, zero) for j in range(3)] for i in range(3)])
            else:
                tail = chain([get18(r) for r in cyc[ROW - n :]])
                put18(tail_ref, tail)
                put18(row_ref, product(tail, head))


def holonomy_kernel(head_ref, row_ref, tail_ref, out_hbm, o_ref, sem):
    loop = product(product(get18(head_ref), get18(row_ref)), get18(tail_ref))
    put18(tiles(o_ref, (2, 3, 3)), loop)
    copies = []
    for h in range(2):
        copies.append(pltpu.make_async_copy(o_ref.at[h], out_hbm.at[h], sem.at[h]))
    for c in copies:
        c.start()
    for c in copies:
        c.wait()


def call(kernel, outs, args, scratch=(), aliases=None, us=1.0):
    def spec(kind):
        return pl.BlockSpec(memory_space=VMEM if kind == "v" else pltpu.HBM)

    shapes = [VMEM(s, F32) if kind == "v" else jax.ShapeDtypeStruct(s, F32) for kind, s in outs]
    values = [pltpu.with_memory_space_constraint(x, VMEM if kind == "v" else pltpu.HBM) for kind, x in args]
    return pl.pallas_call(
        kernel,
        out_shape=shapes,
        in_specs=[spec(k) for k, _ in args],
        out_specs=[spec(k) for k, _ in outs],
        scratch_shapes=list(scratch),
        input_output_aliases=aliases or {},
        compiler_params=pltpu.CompilerParams(vmem_limit_bytes=24 << 20),
        cost_estimate=pl.CostEstimate(flops=int(us * 1e6), bytes_accessed=int(us * 3e6), transcendentals=0),
    )(*values)


def from_ahead(x, axis, k):
    n = lax.axis_size(axis)
    return lax.ppermute(x, axis, [(i, (i - k) % n) for i in range(n)])


def diagonal(x):
    n, k = lax.axis_size("space"), lax.axis_size("tm")
    pairs = [(i * k + j, (i + 1) % n * k + (j - 1) % k) for i in range(n) for j in range(k)]
    return lax.ppermute(x, ("space", "tm"), pairs)


def in_row(x, k):
    n = lax.axis_size("tm")
    return lax.ppermute(x, "tm", [(i, i // ROW * ROW + (i - k) % ROW) for i in range(n)])


def plain(x, slices):
    return jnp.swapaxes(x, -3, -2).reshape(*x.shape[: -4 if slices > 1 else -3], slices, 4, 256)


def program(gauge_links):
    dma = pltpu.SemaphoreType.DMA
    whole = (4, 2, 3, 3, 4, 2, 4, 128)
    mat18 = ("v", (2, 3, 3, 8, 128))
    full = ("h", whole)
    gauge_links = jnp.swapaxes(gauge_links.reshape(4, 2, 3, 3, 4, 4, 2, 128), 5, 6)

    def pack(n):
        return ("v", (n, 8, 128))

    u, st, lowt, low, high, corner = call(
        load_kernel,
        [("v", whole), pack(36), pack(12), pack(24), pack(48), ("v", (24, 128))],
        [("h", gauge_links)],
        [dma(())],
    )
    high = ("v", from_ahead(high, "space", -1))
    corner = ("v", diagonal(corner))
    ht = ("v", from_ahead(st, "tm", 1))
    lowt = ("v", from_ahead(lowt, "space", 1))
    low = ("v", from_ahead(low, "space", 1))
    acc = [("v", (4, 8, 4, 8, 128)), ("v", (4, 8, 5, 8, 128))]
    slices = ("v", (2, 3, 3, 4, 2, 4, 128))
    sums = ("v", (8, 4, 8, 128))
    u, c, r, f, d, up = call(
        steep_kernel,
        [("v", whole), *acc, sums, ("v", (4, 2, 3, 3, 8, 128)), ("v", (3, 2, 3, 3, 8, 128))],
        [("v", u)],
        (),
        {0: 0},
        us=1.5,
    )
    u = ("v", u)
    c, r, f, uz4 = call(
        top_kernel, [*acc, sums, mat18], [u, ht, ("v", d), ("v", up), ("v", c), ("v", r), ("v", f)], (), {4: 0, 5: 1, 6: 2}, us=0.4
    )
    ft, ab, zt, nt, s = call(
        time_kernel,
        [pack(24), pack(16), slices, slices, mat18],
        [u, ("v", uz4), lowt, high, corner, ("v", d), ("v", f), ("v", r)],
        [VMEM((8, 32, 128), F32), VMEM((2, 3, 3, 8, 128), F32), VMEM((8, 8, 128), F32)],
        us=0.6,
    )
    s1, s3, s2 = in_row(s, 1), in_row(s, 3), in_row(s, 2)
    ft = ("v", from_ahead(ft, "tm", -1))
    edges = ("v", (32, 32, 128))
    c, r, x = call(
        flat_kernel,
        [*acc, edges],
        [u, low, high, ("v", ab), ("v", c), ("v", r), ("v", s)],
        [VMEM((2, 2, 3, 3, 32, 128), F32)],
        {4: 0, 5: 1},
        us=2.2,
    )
    head, tail, row = call(join_kernel, [mat18] * 3, [("v", s), ("v", s1), ("v", s2), ("v", s3)], us=0.1)
    row = from_ahead(row, "tm", ROW)

    def stage(count):
        return [VMEM((3, 2, 3, 3, count, 2, 4, 128), F32)] * 2 + [dma((8, 2))]

    shared = [u, ("v", x), ("v", c), ("v", r)]
    new, force = call(space_kernel, [full, full], [*shared, ("v", zt), ("v", nt)], stage(3), us=1.6)
    new, force = call(first_kernel, [full, full], [*shared, ft, ("h", new), ("h", force)], stage(1), {5: 0, 6: 1}, us=1.0)
    (hol,) = call(
        holonomy_kernel,
        [("h", (2, 3, 3, 2, 4, 128))],
        [("v", head), ("v", row), ("v", tail)],
        [VMEM((2, 3, 3, 2, 4, 128), F32), dma((2,))],
    )
    return plain(new, 4), plain(force, 4), plain(hol, 1)


def solution(mesh):
    in_specs = (P(None, None, None, None, "tm", "space", None),)
    out_specs = (
        P(None, None, None, None, "tm", "space", None),
        P(None, None, None, None, "tm", "space", None),
        P(None, None, None, "tm", "space", None),
    )
    return jax.shard_map(program, mesh=mesh, in_specs=in_specs, out_specs=out_specs, check_vma=False)
```

profile of v0, /device:TPU:0, one launch (start us, length us, event | category | flops | bytes accessed | tf_op | source)
XLA Modules:
  0.0 32.8 jit_solution(12411193552314392904)
XLA Ops:
  0.6 1.2 %shard_map.38 = (f32[4,2,3,3,4,2,4,128]{7,6,5,4,3,2,1,0:T(4,128)S(1)}, f32[36,8,128]{2,1,0:T(8,128)S(1)}, f32[12,8,128]{2,1,0:T(8,128)S(1)}, f32[24,8,128]{2,1,0...) custom-call(f32[4,2,3,3,4,2,4,128]{7,6,5,4,3,2,1,0:T(4,128)} %bitcast.12), custom_call_target="tpu_custom_call" | custom-call | flops 1000000 | bytes 3000000 | tf_op jit(solution)/shard_map/pallas_call | solution.py:549
  1.8 0.1 collective-permute-start.1
  1.9 4.0 %collective-permute-start.2 = (f32[36,8,128]{2,1,0:T(8,128)S(1)}, f32[36,8,128]{2,1,0:T(8,128)S(1)}, u32[]{:S(2)}, u32[]{:S(2)}) collective-permute-start(f32[36,8,128]{2,1,0:T(8,128)S(1)} %get-tuple-element.38), channel_id=1, source_target_pairs={{0,7},{1,0},{2,1},{3,2},{4,3},{5,4},{6,5},{7,6},{8,15},{9,8},{10,9... | collective-permute-start | bytes 442376 | tf_op jit(solution)/shard_map/ppermute | solution.py:563
  5.9 5.6 %collective-permute-start.3 = (f32[12,8,128]{2,1,0:T(8,128)S(1)}, f32[12,8,128]{2,1,0:T(8,128)S(1)}, u32[]{:S(2)}, u32[]{:S(2)}) collective-permute-start(f32[12,8,128]{2,1,0:T(8,128)S(1)} %get-tuple-element.45), channel_id=1, source_target_pairs={{0,120},{8,0},{16,8},{24,16},{32,24},{40,32},{48,40},{56,48},{64,5... | collective-permute-start | bytes 147464 | tf_op jit(solution)/shard_map/ppermute | solution.py:563
  11.5 0.0 collective-permute-start.4
  11.5 1.5 %shard_map.39 = (f32[4,2,3,3,4,2,4,128]{7,6,5,4,3,2,1,0:T(4,128)S(1)}, f32[4,8,4,8,128]{4,3,2,1,0:T(8,128)S(1)}, f32[4,8,5,8,128]{4,3,2,1,0:T(8,128)S(1)}, f32[8...) custom-call(f32[4,2,3,3,4,2,4,128]{7,6,5,4,3,2,1,0:T(4,128)S(1)} %ge, ...), custom_call_target="tpu_custom_call", output_to_operand_aliasing={{0}: (0, {})} | custom-call | flops 1500000 | bytes 4500000 | tf_op jit(solution)/shard_map/pallas_call | solution.py:549
  13.0 0.0 collective-permute-done.2.ht_ref
  13.0 0.3 shard_map.40
  13.3 5.8 %collective-permute-done.4.corner_ref = f32[24,128]{1,0:T(8,128)S(1)} collective-permute-done((f32[24,128]{1,0:T(8,128)S(1)}, f32[24,128]{1,0:T(8,128)S(1)}, u32[]{:S(2)}, u32[]{:S(2)}) %collective-permute-start.4) | collective-permute-done | bytes 12320 | tf_op jit(solution)/shard_map/ppermute | solution.py:569
  19.1 0.0 collective-permute-done.3.lowt_ref
  19.1 0.0 collective-permute-done.1.high_ref
  19.1 0.6 %shard_map.41 = (f32[24,8,128]{2,1,0:T(8,128)S(1)}, f32[16,8,128]{2,1,0:T(8,128)S(1)}, f32[2,3,3,4,2,4,128]{6,5,4,3,2,1,0:T(4,128)S(1)}, f32[2,3,3,4,2,4,128]{6,...) custom-call(f32[4,2,3,3,4,2,4,128]{7,6,5,4,3,2,1,0:T(4,128)S(1)} %get-tuple-element.35.u_ref, ...), custom_call_target="tpu_custom_call" | custom-call | flops 600000 | bytes 1800000 | tf_op jit(solution)/shard_map/pallas_call | solution.py:549
  19.7 0.1 collective-permute-start.8
  19.8 2.4 %collective-permute-start.7 = (f32[2,3,3,8,128]{4,3,2,1,0:T(8,128)S(1)}, f32[2,3,3,8,128]{4,3,2,1,0:T(8,128)S(1)}, u32[]{:S(2)}, u32[]{:S(2)}) collective-permute-start(f32[2,3,3,8,128]{4,3,2,1,0:T(8,128)S(1)} %get-tuple-element.51.after_ref.s0_ref), channel_id=1, source_target_pairs={{0,2},{1,3},{2,0},{3,1},{4,6},{5,7},{6,4},{7,5},{8,10},{9,11},{10,... | collective-permute-start | bytes 221192 | tf_op jit(solution)/shard_map/ppermute | solution.py:574
  22.2 0.8 %collective-permute-start.6 = (f32[2,3,3,8,128]{4,3,2,1,0:T(8,128)S(1)}, f32[2,3,3,8,128]{4,3,2,1,0:T(8,128)S(1)}, u32[]{:S(2)}, u32[]{:S(2)}) collective-permute-start(f32[2,3,3,8,128]{4,3,2,1,0:T(8,128)S(1)} %get-tuple-element.51.after_ref.s0_ref), channel_id=1, source_target_pairs={{0,3},{1,0},{2,1},{3,2},{4,7},{5,4},{6,5},{7,6},{8,11},{9,8},{10,9... | collective-permute-start | bytes 221192 | tf_op jit(solution)/shard_map/ppermute | solution.py:574
  23.0 0.0 collective-permute-start
  23.0 1.2 %collective-permute-start.5 = (f32[24,8,128]{2,1,0:T(8,128)S(1)}, f32[24,8,128]{2,1,0:T(8,128)S(1)}, u32[]{:S(2)}, u32[]{:S(2)}) collective-permute-start(f32[24,8,128]{2,1,0:T(8,128)S(1)} %get-tuple-element.55), channel_id=1, source_target_pairs={{0,1},{1,2},{2,3},{3,4},{4,5},{5,6},{6,7},{7,0},{8,9},{9,10},{10,1... | collective-permute-start | bytes 294920 | tf_op jit(solution)/shard_map/ppermute | solution.py:563
  24.2 1.9 %collective-permute-done.8.s3_ref = f32[2,3,3,8,128]{4,3,2,1,0:T(8,128)S(1)} collective-permute-done((f32[2,3,3,8,128]{4,3,2,1,0:T(8,128)S(1)}, f32[2,3,3,8,128]{4,3,2,1,0:T(8,128)S(1)}, u32[]{:S(2)}, u32[]{:S(2)}) %collective-permute-start.8) | collective-permute-done | bytes 73760 | tf_op jit(solution)/shard_map/ppermute | solution.py:574
  26.1 0.0 collective-permute-done.7.s2_ref
  26.1 0.9 %collective-permute-done.6.s1_ref = f32[2,3,3,8,128]{4,3,2,1,0:T(8,128)S(1)} collective-permute-done((f32[2,3,3,8,128]{4,3,2,1,0:T(8,128)S(1)}, f32[2,3,3,8,128]{4,3,2,1,0:T(8,128)S(1)}, u32[]{:S(2)}, u32[]{:S(2)}) %collective-permute-start.6) | collective-permute-done | bytes 73760 | tf_op jit(solution)/shard_map/ppermute | solution.py:574
  27.0 0.1 shard_map.45
  27.1 0.1 collective-permute-start.9
  27.2 0.0 collective-permute-done.low_ref
  27.2 2.1 %shard_map.42 = (f32[4,8,4,8,128]{4,3,2,1,0:T(8,128)S(1)}, f32[4,8,5,8,128]{4,3,2,1,0:T(8,128)S(1)}, f32[32,32,128]{2,1,0:T(8,128)S(1)}) custom-call(f32[4,2,3,3,4,2,4,128]{7,6,5,4,3,2,1,0:T(4,128)S(1)} %get-tuple-element.35.u_ref, f32[24,8,128]{2,1,0:T(8,128)S(1)} %collective-permute-done.low_ref, ...), custom_call_target="tpu_custom_call", output_to_operand_aliasing={{0}: (4, {}), {1}: (5, {})} | custom-call | flops 2200000 | bytes 6600000 | tf_op jit(solution)/shard_map/pallas_call | solution.py:549
  29.3 1.7 %shard_map.43 = (f32[4,2,3,3,4,2,4,128]{7,6,5,4,3,2,1,0:T(4,128)}, f32[4,2,3,3,4,2,4,128]{7,6,5,4,3,2,1,0:T(4,128)}) custom-call(f32[4,2,3,3,4,2,4,128]{7,6,5,4,3,2,1,0:T(4,128)S(1)} %get-tuple-element.35.u_ref, f32[32,32,128]{2,1,0:T(8,128)S(1)} %get-tuple-element.52.x_ref, f32[4,8,4,8,128]{4,3,2,1,0:T(8,128)S(1)} %get-tuple-element.53.c_ref, ...), custom_call_target="tpu_custom_call" | custom-call | flops 1600000 | bytes 4800000 | tf_op jit(solution)/shard_map/pallas_call | solution.py:549
  31.0 0.0 collective-permute-done.5.ft_ref
  31.0 1.0 %shard_map.44 = (f32[4,2,3,3,4,2,4,128]{7,6,5,4,3,2,1,0:T(4,128)}, f32[4,2,3,3,4,2,4,128]{7,6,5,4,3,2,1,0:T(4,128)}) custom-call(f32[4,2,3,3,4,2,4,128]{7,6,5,4,3,2,1,0:T(4,128)S(1)} %get-tuple-element.35.u_ref, f32[32,32,128]{2,1,0:T(8,128)S(1)} %get-tuple-element.52.x_ref, ...), custom_call_target="tpu_custom_call", output_to_operand_aliasing={{0}: (5, {}), {1}: (6, {})} | custom-call | flops 1000000 | bytes 3000000 | tf_op jit(solution)/shard_map/pallas_call | solution.py:549
  32.1 0.0 collective-permute-done.9.row_ref
  32.1 0.7 %shard_map.46 = f32[2,3,3,2,4,128]{5,4,3,2,1,0:T(4,128)} custom-call(f32[2,3,3,8,128]{4,3,2,1,0:T(8,128)S(1)} %get-tuple-element.62.head_ref, f32[2,3,3,8,128]{4,3,2,1,0:T(8,128)S(1)} %collective-permute-done.9.row_ref, f32[2,3,3,8,128]{4,3,2,1,0:T(8,128)S(1)} %get-tuple-element.64.tail_ref), custom_call_target="tpu_custom_call" | custom-call | flops 1000000 | bytes 3000000 | tf_op jit(solution)/shard_map/pallas_call | solution.py:549
Async XLA Ops:
  1.8 17.3 %collective-permute-start.1 = (f32[48,8,128]{2,1,0:T(8,128)S(1)}, f32[48,8,128]{2,1,0:T(8,128)S(1)}, u32[]{:S(2)}, u32[]{:S(2)}) collective-permute-start(f32[48,8,128]{2,1,0:T(8,128)S(1)} %get-tuple-element.37), channel_id=1, source_target_pairs={{0,8},{8,16},{16,24},{24,32},{32,40},{40,48},{48,56},{56,64},{64,7... | collective-permute-start | bytes 589832 | tf_op jit(solution)/shard_map/ppermute | solution.py:563
  1.9 11.1 %collective-permute-start.2 = (f32[36,8,128]{2,1,0:T(8,128)S(1)}, f32[36,8,128]{2,1,0:T(8,128)S(1)}, u32[]{:S(2)}, u32[]{:S(2)}) collective-permute-start(f32[36,8,128]{2,1,0:T(8,128)S(1)} %get-tuple-element.38), channel_id=1, source_target_pairs={{0,7},{1,0},{2,1},{3,2},{4,3},{5,4},{6,5},{7,6},{8,15},{9,8},{10,9... | collective-permute-start | bytes 442376 | tf_op jit(solution)/shard_map/ppermute | solution.py:563
  5.9 13.2 %collective-permute-start.3 = (f32[12,8,128]{2,1,0:T(8,128)S(1)}, f32[12,8,128]{2,1,0:T(8,128)S(1)}, u32[]{:S(2)}, u32[]{:S(2)}) collective-permute-start(f32[12,8,128]{2,1,0:T(8,128)S(1)} %get-tuple-element.45), channel_id=1, source_target_pairs={{0,120},{8,0},{16,8},{24,16},{32,24},{40,32},{48,40},{56,48},{64,5... | collective-permute-start | bytes 147464 | tf_op jit(solution)/shard_map/ppermute | solution.py:563
  11.5 7.6 %collective-permute-start.4 = (f32[24,128]{1,0:T(8,128)S(1)}, f32[24,128]{1,0:T(8,128)S(1)}, u32[]{:S(2)}, u32[]{:S(2)}) collective-permute-start(f32[24,128]{1,0:T(8,128)S(1)} %get-tuple-element.46), channel_id=1, source_target_pairs={{0,15},{1,8},{2,9},{3,10},{4,11},{5,12},{6,13},{7,14},{8,23},{9,16... | collective-permute-start | bytes 36872 | tf_op jit(solution)/shard_map/ppermute | solution.py:569
  19.7 6.4 %collective-permute-start.8 = (f32[2,3,3,8,128]{4,3,2,1,0:T(8,128)S(1)}, f32[2,3,3,8,128]{4,3,2,1,0:T(8,128)S(1)}, u32[]{:S(2)}, u32[]{:S(2)}) collective-permute-start(f32[2,3,3,8,128]{4,3,2,1,0:T(8,128)S(1)} %get-tuple-element.51.after_ref.s0_ref), channel_id=1, source_target_pairs={{0,1},{1,2},{2,3},{3,0},{4,5},{5,6},{6,7},{7,4},{8,9},{9,10},{10,1... | collective-permute-start | bytes 221192 | tf_op jit(solution)/shard_map/ppermute | solution.py:574
  19.8 6.3 %collective-permute-start.7 = (f32[2,3,3,8,128]{4,3,2,1,0:T(8,128)S(1)}, f32[2,3,3,8,128]{4,3,2,1,0:T(8,128)S(1)}, u32[]{:S(2)}, u32[]{:S(2)}) collective-permute-start(f32[2,3,3,8,128]{4,3,2,1,0:T(8,128)S(1)} %get-tuple-element.51.after_ref.s0_ref), channel_id=1, source_target_pairs={{0,2},{1,3},{2,0},{3,1},{4,6},{5,7},{6,4},{7,5},{8,10},{9,11},{10,... | collective-permute-start | bytes 221192 | tf_op jit(solution)/shard_map/ppermute | solution.py:574
  22.2 4.8 %collective-permute-start.6 = (f32[2,3,3,8,128]{4,3,2,1,0:T(8,128)S(1)}, f32[2,3,3,8,128]{4,3,2,1,0:T(8,128)S(1)}, u32[]{:S(2)}, u32[]{:S(2)}) collective-permute-start(f32[2,3,3,8,128]{4,3,2,1,0:T(8,128)S(1)} %get-tuple-element.51.after_ref.s0_ref), channel_id=1, source_target_pairs={{0,3},{1,0},{2,1},{3,2},{4,7},{5,4},{6,5},{7,6},{8,11},{9,8},{10,9... | collective-permute-start | bytes 221192 | tf_op jit(solution)/shard_map/ppermute | solution.py:574
  23.0 4.2 %collective-permute-start = (f32[24,8,128]{2,1,0:T(8,128)S(1)}, f32[24,8,128]{2,1,0:T(8,128)S(1)}, u32[]{:S(2)}, u32[]{:S(2)}) collective-permute-start(f32[24,8,128]{2,1,0:T(8,128)S(1)} %get-tuple-element.36), channel_id=1, source_target_pairs={{0,120},{8,0},{16,8},{24,16},{32,24},{40,32},{48,40},{56,48},{64,5... | collective-permute-start | bytes 294920 | tf_op jit(solution)/shard_map/ppermute | solution.py:563
  23.0 8.0 %collective-permute-start.5 = (f32[24,8,128]{2,1,0:T(8,128)S(1)}, f32[24,8,128]{2,1,0:T(8,128)S(1)}, u32[]{:S(2)}, u32[]{:S(2)}) collective-permute-start(f32[24,8,128]{2,1,0:T(8,128)S(1)} %get-tuple-element.55), channel_id=1, source_target_pairs={{0,1},{1,2},{2,3},{3,4},{4,5},{5,6},{6,7},{7,0},{8,9},{9,10},{10,1... | collective-permute-start | bytes 294920 | tf_op jit(solution)/shard_map/ppermute | solution.py:563
  27.1 5.0 %collective-permute-start.9 = (f32[2,3,3,8,128]{4,3,2,1,0:T(8,128)S(1)}, f32[2,3,3,8,128]{4,3,2,1,0:T(8,128)S(1)}, u32[]{:S(2)}, u32[]{:S(2)}) collective-permute-start(f32[2,3,3,8,128]{4,3,2,1,0:T(8,128)S(1)} %get-tuple-element.63), channel_id=1, source_target_pairs={{0,4},{1,5},{2,6},{3,7},{4,0},{5,1},{6,2},{7,3},{8,12},{9,13},{10,... | collective-permute-start | bytes 221192 | tf_op jit(solution)/shard_map/ppermute | solution.py:563
where the time goes:
time: 33.2 us; the launch traced here: 32.8 us
  starting transfers between devices  14.3 us (43%)
  Pallas kernels  9.19 us (28%)
  waiting for transfers between devices  8.61 us (26%)
  between operations  0.73 us (2%)
    ppermute x6, starting transfers between devices, from_ahead(): return lax.ppermute(x, axis, [(i, (i - k) % n) for i in range(n)])  11 us
    pallas_call x9, Pallas kernels, call(): pl.pallas_call(kernel, out_shape=shapes, in_specs=[spec(k) for k, _ in ar...  9.19 us
    ppermute x1, waiting for transfers between devices, diagonal(): return lax.ppermute(x, ('space', 'tm'), pairs)  5.83 us
    ppermute x3, starting transfers between devices, in_row(): lax.ppermute(x, 'tm', [(i, i // ROW * ROW + (i - k) % ROW) for i in range...  3.3 us
    ppermute x3, waiting for transfers between devices, in_row(): lax.ppermute(x, 'tm', [(i, i // ROW * ROW + (i - k) % ROW) for i in range...  2.76 us
  transfers between devices with their start and end apart: 10, of which 3 were waited for; matrix products, arithmetic and copies ran while one was open for 0% of the time, Pallas kernels for 20%

commit v1 on v0

--- a/solution.py
+++ b/solution.py
@@ -202,12 +202,13 @@
 
 def load_kernel(u_hbm, u_ref, st_ref, lowt_ref, low_ref, high_ref, corner_ref, sem):
     two = pl.ds(0, 2)
-    copy = pltpu.make_async_copy(u_hbm.at[:, :, two], u_ref.at[:, :, two], sem)
-    copy.start()
-    copy.wait()
+    copies = [pltpu.make_async_copy(u_hbm.at[d, :, two], u_ref.at[d, :, two], sem.at[d]) for d in range(4)]
+    for copy in copies:
+        copy.start()
     u = tiles(u_ref, (4, 2, 3, 3, 4))
     rows = u_ref.reshape(4, 2, 3, 3, 32, 128)
     for d in range(4):
+        copies[d].wait()
         for p in range(2):
             for i in range(2):
                 for j in range(3):
@@ -592,7 +593,7 @@
         load_kernel,
         [("v", whole), pack(36), pack(12), pack(24), pack(48), ("v", (24, 128))],
         [("h", gauge_links)],
-        [dma(())],
+        [dma((4,))],
     )
     high = ("v", from_ahead(high, "space", -1))
     corner = ("v", diagonal(corner))

time: 33.2 us -> 33.3 us (level)
  no operation moved by 1% of the time
where the time goes in v1:
time: 33.3 us; the launch traced here: 32.9 us
  starting transfers between devices  14.3 us (43%)
  Pallas kernels  9.26 us (28%)
  waiting for transfers between devices  8.61 us (26%)
  between operations  0.73 us (2%)
    ppermute x6, starting transfers between devices, from_ahead(): return lax.ppermute(x, axis, [(i, (i - k) % n) for i in range(n)])  11 us
    pallas_call x9, Pallas kernels, call(): pl.pallas_call(kernel, out_shape=shapes, in_specs=[spec(k) for k, _ in ar...  9.26 us
    ppermute x1, waiting for transfers between devices, diagonal(): return lax.ppermute(x, ('space', 'tm'), pairs)  5.83 us
    ppermute x3, starting transfers between devices, in_row(): lax.ppermute(x, 'tm', [(i, i // ROW * ROW + (i - k) % ROW) for i in range...  3.3 us
    ppermute x3, waiting for transfers between devices, in_row(): lax.ppermute(x, 'tm', [(i, i // ROW * ROW + (i - k) % ROW) for i in range...  2.76 us
  transfers between devices with their start and end apart: 10, of which 3 were waited for; matrix products, arithmetic and copies ran while one was open for 0% of the time, Pallas kernels for 20%

profile of v1, /device:TPU:0, one launch (start us, length us, event | category | flops | bytes accessed | tf_op | source)
XLA Modules:
  0.0 32.9 jit_solution(16673775034554929678)
XLA Ops:
  0.6 1.3 %shard_map.38 = (f32[4,2,3,3,4,2,4,128]{7,6,5,4,3,2,1,0:T(4,128)S(1)}, f32[36,8,128]{2,1,0:T(8,128)S(1)}, f32[12,8,128]{2,1,0:T(8,128)S(1)}, f32[24,8,128]{2,1,0...) custom-call(f32[4,2,3,3,4,2,4,128]{7,6,5,4,3,2,1,0:T(4,128)} %bitcast.12), custom_call_target="tpu_custom_call" | custom-call | flops 1000000 | bytes 3000000 | tf_op jit(solution)/shard_map/pallas_call | solution.py:550
  1.9 0.1 collective-permute-start.1
  2.0 4.0 %collective-permute-start.2 = (f32[36,8,128]{2,1,0:T(8,128)S(1)}, f32[36,8,128]{2,1,0:T(8,128)S(1)}, u32[]{:S(2)}, u32[]{:S(2)}) collective-permute-start(f32[36,8,128]{2,1,0:T(8,128)S(1)} %get-tuple-element.38), channel_id=1, source_target_pairs={{0,7},{1,0},{2,1},{3,2},{4,3},{5,4},{6,5},{7,6},{8,15},{9,8},{10,9... | collective-permute-start | bytes 442376 | tf_op jit(solution)/shard_map/ppermute | solution.py:564
  5.9 5.6 %collective-permute-start.3 = (f32[12,8,128]{2,1,0:T(8,128)S(1)}, f32[12,8,128]{2,1,0:T(8,128)S(1)}, u32[]{:S(2)}, u32[]{:S(2)}) collective-permute-start(f32[12,8,128]{2,1,0:T(8,128)S(1)} %get-tuple-element.45), channel_id=1, source_target_pairs={{0,120},{8,0},{16,8},{24,16},{32,24},{40,32},{48,40},{56,48},{64,5... | collective-permute-start | bytes 147464 | tf_op jit(solution)/shard_map/ppermute | solution.py:564
  11.5 0.0 collective-permute-start.4
  11.5 1.5 %shard_map.39 = (f32[4,2,3,3,4,2,4,128]{7,6,5,4,3,2,1,0:T(4,128)S(1)}, f32[4,8,4,8,128]{4,3,2,1,0:T(8,128)S(1)}, f32[4,8,5,8,128]{4,3,2,1,0:T(8,128)S(1)}, f32[8...) custom-call(f32[4,2,3,3,4,2,4,128]{7,6,5,4,3,2,1,0:T(4,128)S(1)} %ge, ...), custom_call_target="tpu_custom_call", output_to_operand_aliasing={{0}: (0, {})} | custom-call | flops 1500000 | bytes 4500000 | tf_op jit(solution)/shard_map/pallas_call | solution.py:550
  13.0 0.0 collective-permute-done.2.ht_ref
  13.1 0.3 shard_map.40
  13.3 5.8 %collective-permute-done.4.corner_ref = f32[24,128]{1,0:T(8,128)S(1)} collective-permute-done((f32[24,128]{1,0:T(8,128)S(1)}, f32[24,128]{1,0:T(8,128)S(1)}, u32[]{:S(2)}, u32[]{:S(2)}) %collective-permute-start.4) | collective-permute-done | bytes 12320 | tf_op jit(solution)/shard_map/ppermute | solution.py:570
  19.2 0.0 collective-permute-done.3.lowt_ref
  19.2 0.0 collective-permute-done.1.high_ref
  19.2 0.6 %shard_map.41 = (f32[24,8,128]{2,1,0:T(8,128)S(1)}, f32[16,8,128]{2,1,0:T(8,128)S(1)}, f32[2,3,3,4,2,4,128]{6,5,4,3,2,1,0:T(4,128)S(1)}, f32[2,3,3,4,2,4,128]{6,...) custom-call(f32[4,2,3,3,4,2,4,128]{7,6,5,4,3,2,1,0:T(4,128)S(1)} %get-tuple-element.35.u_ref, ...), custom_call_target="tpu_custom_call" | custom-call | flops 600000 | bytes 1800000 | tf_op jit(solution)/shard_map/pallas_call | solution.py:550
  19.8 0.1 collective-permute-start.8
  19.8 2.4 %collective-permute-start.7 = (f32[2,3,3,8,128]{4,3,2,1,0:T(8,128)S(1)}, f32[2,3,3,8,128]{4,3,2,1,0:T(8,128)S(1)}, u32[]{:S(2)}, u32[]{:S(2)}) collective-permute-start(f32[2,3,3,8,128]{4,3,2,1,0:T(8,128)S(1)} %get-tuple-element.51.after_ref.s0_ref), channel_id=1, source_target_pairs={{0,2},{1,3},{2,0},{3,1},{4,6},{5,7},{6,4},{7,5},{8,10},{9,11},{10,... | collective-permute-start | bytes 221192 | tf_op jit(solution)/shard_map/ppermute | solution.py:575
  22.2 0.8 %collective-permute-start.6 = (f32[2,3,3,8,128]{4,3,2,1,0:T(8,128)S(1)}, f32[2,3,3,8,128]{4,3,2,1,0:T(8,128)S(1)}, u32[]{:S(2)}, u32[]{:S(2)}) collective-permute-start(f32[2,3,3,8,128]{4,3,2,1,0:T(8,128)S(1)} %get-tuple-element.51.after_ref.s0_ref), channel_id=1, source_target_pairs={{0,3},{1,0},{2,1},{3,2},{4,7},{5,4},{6,5},{7,6},{8,11},{9,8},{10,9... | collective-permute-start | bytes 221192 | tf_op jit(solution)/shard_map/ppermute | solution.py:575
  23.1 0.0 collective-permute-start
  23.1 1.2 %collective-permute-start.5 = (f32[24,8,128]{2,1,0:T(8,128)S(1)}, f32[24,8,128]{2,1,0:T(8,128)S(1)}, u32[]{:S(2)}, u32[]{:S(2)}) collective-permute-start(f32[24,8,128]{2,1,0:T(8,128)S(1)} %get-tuple-element.55), channel_id=1, source_target_pairs={{0,1},{1,2},{2,3},{3,4},{4,5},{5,6},{6,7},{7,0},{8,9},{9,10},{10,1... | collective-permute-start | bytes 294920 | tf_op jit(solution)/shard_map/ppermute | solution.py:564
  24.3 1.9 %collective-permute-done.8.s3_ref = f32[2,3,3,8,128]{4,3,2,1,0:T(8,128)S(1)} collective-permute-done((f32[2,3,3,8,128]{4,3,2,1,0:T(8,128)S(1)}, f32[2,3,3,8,128]{4,3,2,1,0:T(8,128)S(1)}, u32[]{:S(2)}, u32[]{:S(2)}) %collective-permute-start.8) | collective-permute-done | bytes 73760 | tf_op jit(solution)/shard_map/ppermute | solution.py:575
  26.2 0.0 collective-permute-done.7.s2_ref
  26.2 0.9 %collective-permute-done.6.s1_ref = f32[2,3,3,8,128]{4,3,2,1,0:T(8,128)S(1)} collective-permute-done((f32[2,3,3,8,128]{4,3,2,1,0:T(8,128)S(1)}, f32[2,3,3,8,128]{4,3,2,1,0:T(8,128)S(1)}, u32[]{:S(2)}, u32[]{:S(2)}) %collective-permute-start.6) | collective-permute-done | bytes 73760 | tf_op jit(solution)/shard_map/ppermute | solution.py:575
  27.0 0.1 shard_map.45
  27.1 0.1 collective-permute-start.9
  27.3 0.0 collective-permute-done.low_ref
  27.3 2.1 %shard_map.42 = (f32[4,8,4,8,128]{4,3,2,1,0:T(8,128)S(1)}, f32[4,8,5,8,128]{4,3,2,1,0:T(8,128)S(1)}, f32[32,32,128]{2,1,0:T(8,128)S(1)}) custom-call(f32[4,2,3,3,4,2,4,128]{7,6,5,4,3,2,1,0:T(4,128)S(1)} %get-tuple-element.35.u_ref, f32[24,8,128]{2,1,0:T(8,128)S(1)} %collective-permute-done.low_ref, ...), custom_call_target="tpu_custom_call", output_to_operand_aliasing={{0}: (4, {}), {1}: (5, {})} | custom-call | flops 2200000 | bytes 6600000 | tf_op jit(solution)/shard_map/pallas_call | solution.py:550
  29.4 1.7 %shard_map.43 = (f32[4,2,3,3,4,2,4,128]{7,6,5,4,3,2,1,0:T(4,128)}, f32[4,2,3,3,4,2,4,128]{7,6,5,4,3,2,1,0:T(4,128)}) custom-call(f32[4,2,3,3,4,2,4,128]{7,6,5,4,3,2,1,0:T(4,128)S(1)} %get-tuple-element.35.u_ref, f32[32,32,128]{2,1,0:T(8,128)S(1)} %get-tuple-element.52.x_ref, f32[4,8,4,8,128]{4,3,2,1,0:T(8,128)S(1)} %get-tuple-element.53.c_ref, ...), custom_call_target="tpu_custom_call" | custom-call | flops 1600000 | bytes 4800000 | tf_op jit(solution)/shard_map/pallas_call | solution.py:550
  31.1 0.0 collective-permute-done.5.ft_ref
  31.1 1.0 %shard_map.44 = (f32[4,2,3,3,4,2,4,128]{7,6,5,4,3,2,1,0:T(4,128)}, f32[4,2,3,3,4,2,4,128]{7,6,5,4,3,2,1,0:T(4,128)}) custom-call(f32[4,2,3,3,4,2,4,128]{7,6,5,4,3,2,1,0:T(4,128)S(1)} %get-tuple-element.35.u_ref, f32[32,32,128]{2,1,0:T(8,128)S(1)} %get-tuple-element.52.x_ref, ...), custom_call_target="tpu_custom_call", output_to_operand_aliasing={{0}: (5, {}), {1}: (6, {})} | custom-call | flops 1000000 | bytes 3000000 | tf_op jit(solution)/shard_map/pallas_call | solution.py:550
  32.2 0.0 collective-permute-done.9.row_ref
  32.2 0.7 %shard_map.46 = f32[2,3,3,2,4,128]{5,4,3,2,1,0:T(4,128)} custom-call(f32[2,3,3,8,128]{4,3,2,1,0:T(8,128)S(1)} %get-tuple-element.62.head_ref, f32[2,3,3,8,128]{4,3,2,1,0:T(8,128)S(1)} %collective-permute-done.9.row_ref, f32[2,3,3,8,128]{4,3,2,1,0:T(8,128)S(1)} %get-tuple-element.64.tail_ref), custom_call_target="tpu_custom_call" | custom-call | flops 1000000 | bytes 3000000 | tf_op jit(solution)/shard_map/pallas_call | solution.py:550
Async XLA Ops:
  1.9 17.3 %collective-permute-start.1 = (f32[48,8,128]{2,1,0:T(8,128)S(1)}, f32[48,8,128]{2,1,0:T(8,128)S(1)}, u32[]{:S(2)}, u32[]{:S(2)}) collective-permute-start(f32[48,8,128]{2,1,0:T(8,128)S(1)} %get-tuple-element.37), channel_id=1, source_target_pairs={{0,8},{8,16},{16,24},{24,32},{32,40},{40,48},{48,56},{56,64},{64,7... | collective-permute-start | bytes 589832 | tf_op jit(solution)/shard_map/ppermute | solution.py:564
  2.0 11.1 %collective-permute-start.2 = (f32[36,8,128]{2,1,0:T(8,128)S(1)}, f32[36,8,128]{2,1,0:T(8,128)S(1)}, u32[]{:S(2)}, u32[]{:S(2)}) collective-permute-start(f32[36,8,128]{2,1,0:T(8,128)S(1)} %get-tuple-element.38), channel_id=1, source_target_pairs={{0,7},{1,0},{2,1},{3,2},{4,3},{5,4},{6,5},{7,6},{8,15},{9,8},{10,9... | collective-permute-start | bytes 442376 | tf_op jit(solution)/shard_map/ppermute | solution.py:564
  5.9 13.2 %collective-permute-start.3 = (f32[12,8,128]{2,1,0:T(8,128)S(1)}, f32[12,8,128]{2,1,0:T(8,128)S(1)}, u32[]{:S(2)}, u32[]{:S(2)}) collective-permute-start(f32[12,8,128]{2,1,0:T(8,128)S(1)} %get-tuple-element.45), channel_id=1, source_target_pairs={{0,120},{8,0},{16,8},{24,16},{32,24},{40,32},{48,40},{56,48},{64,5... | collective-permute-start | bytes 147464 | tf_op jit(solution)/shard_map/ppermute | solution.py:564
  11.5 7.6 %collective-permute-start.4 = (f32[24,128]{1,0:T(8,128)S(1)}, f32[24,128]{1,0:T(8,128)S(1)}, u32[]{:S(2)}, u32[]{:S(2)}) collective-permute-start(f32[24,128]{1,0:T(8,128)S(1)} %get-tuple-element.46), channel_id=1, source_target_pairs={{0,15},{1,8},{2,9},{3,10},{4,11},{5,12},{6,13},{7,14},{8,23},{9,16... | collective-permute-start | bytes 36872 | tf_op jit(solution)/shard_map/ppermute | solution.py:570
  19.8 6.4 %collective-permute-start.8 = (f32[2,3,3,8,128]{4,3,2,1,0:T(8,128)S(1)}, f32[2,3,3,8,128]{4,3,2,1,0:T(8,128)S(1)}, u32[]{:S(2)}, u32[]{:S(2)}) collective-permute-start(f32[2,3,3,8,128]{4,3,2,1,0:T(8,128)S(1)} %get-tuple-element.51.after_ref.s0_ref), channel_id=1, source_target_pairs={{0,1},{1,2},{2,3},{3,0},{4,5},{5,6},{6,7},{7,4},{8,9},{9,10},{10,1... | collective-permute-start | bytes 221192 | tf_op jit(solution)/shard_map/ppermute | solution.py:575
  19.8 6.3 %collective-permute-start.7 = (f32[2,3,3,8,128]{4,3,2,1,0:T(8,128)S(1)}, f32[2,3,3,8,128]{4,3,2,1,0:T(8,128)S(1)}, u32[]{:S(2)}, u32[]{:S(2)}) collective-permute-start(f32[2,3,3,8,128]{4,3,2,1,0:T(8,128)S(1)} %get-tuple-element.51.after_ref.s0_ref), channel_id=1, source_target_pairs={{0,2},{1,3},{2,0},{3,1},{4,6},{5,7},{6,4},{7,5},{8,10},{9,11},{10,... | collective-permute-start | bytes 221192 | tf_op jit(solution)/shard_map/ppermute | solution.py:575
  22.2 4.8 %collective-permute-start.6 = (f32[2,3,3,8,128]{4,3,2,1,0:T(8,128)S(1)}, f32[2,3,3,8,128]{4,3,2,1,0:T(8,128)S(1)}, u32[]{:S(2)}, u32[]{:S(2)}) collective-permute-start(f32[2,3,3,8,128]{4,3,2,1,0:T(8,128)S(1)} %get-tuple-element.51.after_ref.s0_ref), channel_id=1, source_target_pairs={{0,3},{1,0},{2,1},{3,2},{4,7},{5,4},{6,5},{7,6},{8,11},{9,8},{10,9... | collective-permute-start | bytes 221192 | tf_op jit(solution)/shard_map/ppermute | solution.py:575
  23.1 4.2 %collective-permute-start = (f32[24,8,128]{2,1,0:T(8,128)S(1)}, f32[24,8,128]{2,1,0:T(8,128)S(1)}, u32[]{:S(2)}, u32[]{:S(2)}) collective-permute-start(f32[24,8,128]{2,1,0:T(8,128)S(1)} %get-tuple-element.36), channel_id=1, source_target_pairs={{0,120},{8,0},{16,8},{24,16},{32,24},{40,32},{48,40},{56,48},{64,5... | collective-permute-start | bytes 294920 | tf_op jit(solution)/shard_map/ppermute | solution.py:564
  23.1 8.0 %collective-permute-start.5 = (f32[24,8,128]{2,1,0:T(8,128)S(1)}, f32[24,8,128]{2,1,0:T(8,128)S(1)}, u32[]{:S(2)}, u32[]{:S(2)}) collective-permute-start(f32[24,8,128]{2,1,0:T(8,128)S(1)} %get-tuple-element.55), channel_id=1, source_target_pairs={{0,1},{1,2},{2,3},{3,4},{4,5},{5,6},{6,7},{7,0},{8,9},{9,10},{10,1... | collective-permute-start | bytes 294920 | tf_op jit(solution)/shard_map/ppermute | solution.py:564
  27.1 5.0 %collective-permute-start.9 = (f32[2,3,3,8,128]{4,3,2,1,0:T(8,128)S(1)}, f32[2,3,3,8,128]{4,3,2,1,0:T(8,128)S(1)}, u32[]{:S(2)}, u32[]{:S(2)}) collective-permute-start(f32[2,3,3,8,128]{4,3,2,1,0:T(8,128)S(1)} %get-tuple-element.63), channel_id=1, source_target_pairs={{0,4},{1,5},{2,6},{3,7},{4,0},{5,1},{6,2},{7,3},{8,12},{9,13},{10,... | collective-permute-start | bytes 221192 | tf_op jit(solution)/shard_map/ppermute | solution.py:564
